TPU v7x, 768 devices: a whole 4x8x12 slice. The times are simulated.
768 devices in a mesh: rows: 192 (over x, y_lo, z), cols: 4 (over y_hi, core).
Axes of the slice: x: 4, y: 8 (y_hi: 2, y_lo: 4; y = y_hi * 4 + y_lo), z: 12, core: 2. Of those that a mesh axis runs over, the one named last changes fastest.
Arguments:
- row_feat: bfloat16 [3072, 512], P('rows', 'cols'), may hold values from -6 to 6
- col_feat: bfloat16 [4, 192, 512], P('cols', 'rows'), may hold values from -6 to 6
- bucket_ids: int32 [3072, 768], P('rows', 'cols'), may hold values from 0 to 127, as said below
- w_row: bfloat16 [512, 128], replicated, may hold values from -0.25 to 0.25
- w_col: bfloat16 [512, 128], replicated, may hold values from -0.25 to 0.25
- w_out: bfloat16 [128, 128], replicated, may hold values from -0.5 to 0.5
- bias_table: bfloat16 [128, 128], replicated, may hold values from -6 to 6
- kernel_one: bfloat16 [9, 128, 128], replicated, may hold values from -0.1875 to 0.1875
- kernel_two: bfloat16 [9, 128, 128], replicated, may hold values from -0.1875 to 0.1875
Outputs:
- contact: bfloat16 [3072, 768, 128], P('rows', 'cols')
Inputs may be any that keep to these rules, and one draw needn't show every extreme that they name: bucket_ids[i, j] = clip(floor((j - i + 3072 + s) * 5 * 128 / (4 (3840))) - 16, 0, 127), where i and j are global bin indices and s is one whole-number offset of the slab along the chromosome, the same for all pairs, with |s| <= 240.
All inputs are finite; a program needn't handle non-finite values.
Results may differ from a plain program's by a relative error of at most 0.015.
Values may be sent and summed in bfloat16 or wider, within the bound.
A program may use at most 32 MiB of HBM per device.

v0:
```python
import jax
import jax.numpy as jnp
from jax import lax
from jax.sharding import PartitionSpec as P


def with_halo(cells, sides, width):
    for axis, dim in sides:
        count = lax.axis_size(axis)
        ends = count - 1
        head = lax.slice_in_dim(cells, 0, width, axis=dim)
        tail = lax.slice_in_dim(cells, cells.shape[dim] - width, cells.shape[dim], axis=dim)
        cells = jnp.concatenate(
            [
                lax.ppermute(tail, axis, [(i, (i + 1) % count) for i in range(ends)]),
                cells,
                lax.ppermute(head, axis, [((i + 1) % count, i) for i in range(ends)]),
            ],
            axis=dim,
        )
    return cells


def gelu_round(values):
    return jax.nn.gelu(values.astype(jnp.float32)).astype(jnp.bfloat16)


def convolve(padded, kernel, dilation, height, breadth):
    channels = padded.shape[2]
    running = jnp.zeros((height * breadth, channels), jnp.float32)
    for row_tap in range(3):
        for col_tap in range(3):
            window = padded[
                row_tap * dilation : row_tap * dilation + height,
                col_tap * dilation : col_tap * dilation + breadth,
            ]
            running = running + jnp.dot(
                window.reshape(-1, channels),
                kernel[3 * row_tap + col_tap],
                preferred_element_type=jnp.float32,
            )
    return running.reshape(height, breadth, channels)


def per_device(
    row_feat, col_feat, bucket_ids, w_row, w_col, w_out, bias_table, kernel_one, kernel_two
):
    height, breadth = bucket_ids.shape
    channels = w_row.shape[1]
    buckets = bias_table.shape[0]
    row_sums = jnp.dot(
        lax.all_gather(row_feat, "cols", axis=1, tiled=True),
        w_row,
        preferred_element_type=jnp.float32,
    )
    row_proj = row_sums.astype(jnp.bfloat16)
    col_proj = jnp.dot(
        lax.all_gather(col_feat, "rows", axis=1, tiled=True)[0],
        w_col,
        preferred_element_type=jnp.float32,
    ).astype(jnp.bfloat16)[None][0]
    outer = (
        row_proj[:, None, :].astype(jnp.float32) * col_proj[None, :, :].astype(jnp.float32)
    ).astype(jnp.bfloat16)
    onehot = (
        bucket_ids.reshape(-1)[:, None] == jnp.arange(buckets, dtype=jnp.int32)[None, :]
    ).astype(jnp.bfloat16)
    mixed = jnp.dot(outer.reshape(-1, channels), w_out, preferred_element_type=jnp.float32)
    mixed = mixed + jnp.dot(onehot, bias_table, preferred_element_type=jnp.float32)
    pair0 = mixed.astype(jnp.bfloat16).reshape(height, breadth, channels)
    margin_one = with_halo(pair0, (("rows", 0), ("cols", 1)), 2)
    pair1 = (
        pair0.astype(jnp.float32) + convolve(gelu_round(margin_one), kernel_one, 2, height, breadth)
    ).astype(jnp.bfloat16)
    margin_two = with_halo(pair1, (("rows", 0), ("cols", 1)), 4)
    return (
        pair1.astype(jnp.float32) + convolve(gelu_round(margin_two), kernel_two, 4, height, breadth)
    ).astype(jnp.bfloat16)


def solution(mesh):
    in_specs = (
        P("rows", "cols"),
        P("cols", "rows", None),
        P("rows", "cols"),
        P(),
        P(),
        P(),
        P(),
        P(),
        P(),
    )
    out_specs = P("rows", "cols", None)
    return jax.shard_map(
        per_device, mesh=mesh, in_specs=in_specs, out_specs=out_specs, check_vma=False
    )
```

profile of v0, /device:TPU:1, one launch (start us, length us, event | category | flops | bytes accessed | tf_op | source)
XLA Modules:
  0.0 626.9 jit_solution(2779640154696852989)
XLA Ops:
  0.0 0.8 eq.15
  0.8 19.6 %all_gather.6 = bf16[16,512]{1,0:T(8,128)(2,1)S(1)} all-gather(bf16[16,128]{1,0:T(8,128)(2,1)} %param.9), channel_id=1, replica_groups=mesh['rows'=192,'cols'=4] {'cols'}, dimensions={1}, use_global_device_ids=true | all-gather | bytes 20480 | tf_op jit(solution)/shard_map/all_gather | solution.py:52
  20.4 462.9 %all_gather.7 = bf16[1,192,512]{2,0,1:T(2,128)(2,1)S(1)} all-gather(bf16[1,1,512]{2,0,1:T(2,128)(2,1)} %bitcast.132), channel_id=1, replica_groups=mesh['rows'=192,'cols'=4] {'rows'}, dimensions={1}, use_global_device_ids=true | all-gather | bytes 197632 | tf_op jit(solution)/shard_map/all_gather | solution.py:58
  483.3 1.0 fusion.14
  485.3 1.6 fusion
  487.0 1.3 collective-permute-start.1
  488.3 4.0 collective-permute-start
  492.3 1.6 collective-permute-done
  493.9 88.7 %collective-permute-start.2 = (bf16[20,2,128]{2,1,0:T(2,128)(2,1)S(1)}, bf16[20,2,128]{2,1,0:T(2,128)(2,1)S(1)}, u32[]{:S(2)}, u32[]{:S(2)}) collective-permute-start(bf16[20,2,128]{2,1,0:T(2,128)(2,1)S(1)} %get-tuple-element.25), channel_id=1, source_target_pairs={{0,1},{1,2},{2,3},{4,5},{5,6},{6,7},{8,9},{9,10},{10,11},{12,13},{... | collective-permute-start | bytes 30728 | tf_op jit(solution)/shard_map/ppermute | solution.py:15
  582.6 1.9 collective-permute-start.3
  584.5 7.0 %collective-permute-done.3 = bf16[20,2,128]{2,1,0:T(2,128)(2,1)S(1)} collective-permute-done((bf16[20,2,128]{2,1,0:T(2,128)(2,1)S(1)}, bf16[20,2,128]{2,1,0:T(2,128)(2,1)S(1)}, u32[]{:S(2)}, u32[]{:S(2)}) %collective-permute-start.3) | collective-permute-done | bytes 10272 | tf_op jit(solution)/shard_map/ppermute | solution.py:17
  591.5 1.0 fusion.12
  592.4 1.4 fusion.57
  597.3 4.0 collective-permute-start.4
  601.3 1.3 collective-permute-start.5
  602.6 1.3 collective-permute-done.4
  603.9 3.8 collective-permute-done.5
  607.7 3.4 collective-permute-start.6
  611.1 2.1 collective-permute-start.7
  613.2 6.9 %collective-permute-done.7 = bf16[24,4,128]{2,1,0:T(4,128)(2,1)S(1)} collective-permute-done((bf16[24,4,128]{2,1,0:T(4,128)(2,1)S(1)}, bf16[24,4,128]{2,1,0:T(4,128)(2,1)S(1)}, u32[]{:S(2)}, u32[]{:S(2)}) %collective-permute-start.7) | collective-permute-done | bytes 24608 | tf_op jit(solution)/shard_map/ppermute | solution.py:17
  620.2 1.2 fusion.6
  621.3 1.3 fusion.56
  623.0 0.4 convolution_add_fusion.7
  625.9 1.1 add_convert_fusion
  (38 shorter events, 7.2 us)
Async XLA Ops:
  0.0 484.3 %copy-start = (bf16[512,128]{1,0:T(8,128)(2,1)S(1)}, bf16[512,128]{1,0:T(8,128)(2,1)}, u32[]{:S(2)}) copy-start(bf16[512,128]{1,0:T(8,128)(2,1)} %param.13) | copy-start | bytes 393220
  0.0 484.7 %copy-start.3 = (bf16[128,128]{1,0:T(8,128)(2,1)S(1)}, bf16[128,128]{1,0:T(8,128)(2,1)}, u32[]{:S(2)}) copy-start(bf16[128,128]{1,0:T(8,128)(2,1)} %param.14) | copy-start | bytes 98308
  484.5 0.8 copy-start.4
  487.0 5.4 collective-permute-start.1
  488.3 5.6 collective-permute-start
  493.9 90.6 %collective-permute-start.2 = (bf16[20,2,128]{2,1,0:T(2,128)(2,1)S(1)}, bf16[20,2,128]{2,1,0:T(2,128)(2,1)S(1)}, u32[]{:S(2)}, u32[]{:S(2)}) collective-permute-start(bf16[20,2,128]{2,1,0:T(2,128)(2,1)S(1)} %get-tuple-element.25), channel_id=1, source_target_pairs={{0,1},{1,2},{2,3},{4,5},{5,6},{6,7},{8,9},{9,10},{10,11},{12,13},{... | collective-permute-start | bytes 30728 | tf_op jit(solution)/shard_map/ppermute | solution.py:15
  582.6 8.9 %collective-permute-start.3 = (bf16[20,2,128]{2,1,0:T(2,128)(2,1)S(1)}, bf16[20,2,128]{2,1,0:T(2,128)(2,1)S(1)}, u32[]{:S(2)}, u32[]{:S(2)}) collective-permute-start(bf16[20,2,128]{2,1,0:T(2,128)(2,1)S(1)} %get-tuple-element.26), channel_id=1, source_target_pairs={{1,0},{2,1},{3,2},{5,4},{6,5},{7,6},{9,8},{10,9},{11,10},{13,12},{... | collective-permute-start | bytes 30728 | tf_op jit(solution)/shard_map/ppermute | solution.py:17
  592.4 1.4 copy-start.1
  597.3 6.6 %collective-permute-start.4 = (bf16[4,192,128]{2,1,0:T(8,128)(2,1)S(1)}, bf16[4,192,128]{2,1,0:T(8,128)(2,1)S(1)}, u32[]{:S(2)}, u32[]{:S(2)}) collective-permute-start(bf16[4,192,128]{2,1,0:T(8,128)(2,1)S(1)} %get-tuple-element.27), channel_id=1, source_target_pairs={{0,4},{4,8},{8,12},{12,16},{16,20},{20,24},{24,28},{28,32},{32,36}... | collective-permute-start | bytes 589832 | tf_op jit(solution)/shard_map/ppermute | solution.py:15
  601.3 6.4 %collective-permute-start.5 = (bf16[4,192,128]{2,1,0:T(8,128)(2,1)S(1)}, bf16[4,192,128]{2,1,0:T(8,128)(2,1)S(1)}, u32[]{:S(2)}, u32[]{:S(2)}) collective-permute-start(bf16[4,192,128]{2,1,0:T(8,128)(2,1)S(1)} %get-tuple-element.28), channel_id=1, source_target_pairs={{4,0},{8,4},{12,8},{16,12},{20,16},{24,20},{28,24},{32,28},{36,32}... | collective-permute-start | bytes 589832 | tf_op jit(solution)/shard_map/ppermute | solution.py:17
  607.7 5.5 collective-permute-start.6
  611.1 9.1 %collective-permute-start.7 = (bf16[24,4,128]{2,1,0:T(4,128)(2,1)S(1)}, bf16[24,4,128]{2,1,0:T(4,128)(2,1)S(1)}, u32[]{:S(2)}, u32[]{:S(2)}) collective-permute-start(bf16[24,4,128]{2,1,0:T(4,128)(2,1)S(1)} %get-tuple-element.15), channel_id=1, source_target_pairs={{1,0},{2,1},{3,2},{5,4},{6,5},{7,6},{9,8},{10,9},{11,10},{13,12},{... | collective-permute-start | bytes 73736 | tf_op jit(solution)/shard_map/ppermute | solution.py:17
  621.3 1.3 copy-start.2
where the time goes:
time: 627 us
  blocking collectives  482 us (77%)
  starting transfers between devices  107 us (17%)
  waiting for transfers between devices  20.6 us (3%)
  matrix products  9.45 us (2%)
    all_gather x1, blocking collectives, per_device(): lax.all_gather(col_feat, 'rows', axis=1, tiled=True)[0]  463 us
    ppermute x4, starting transfers between devices, with_halo(): lax.ppermute(tail, axis, [(i, (i + 1) % count) for i in range(ends)])  100 us
    all_gather x1, blocking collectives, per_device(): lax.all_gather(row_feat, 'cols', axis=1, tiled=True)  19.6 us
    ppermute x4, waiting for transfers between devices, with_halo(): lax.ppermute(head, axis, [((i + 1) % count, i) for i in range(ends)])  17.8 us
  transfers between devices with their start and end apart: 8, of which 6 were waited for; matrix products, arithmetic and copies ran while one was open for 0% of the time, Pallas kernels for 0%

commit v1 on v0

v1 whole, which is shorter than its diff:
```python
import functools

import jax
import jax.numpy as jnp
from jax import lax
from jax.experimental import pallas as pl
from jax.experimental.pallas import tpu as pltpu
from jax.sharding import PartitionSpec as P

MESH = pl.DeviceIdType.MESH
F32 = jnp.float32
BF16 = jnp.bfloat16

NX, NY, NZ = 4, 4, 12
NROW, NCOL = NX * NY * NZ, 4
TR, TC, CH = 16, 192, 128
STEP = 24
BASE = 3072
LOW = -240
EXT = 28
WIDE = 208
TAB = 240
CHUNK = 64


def place():
    row, col = lax.axis_index("rows"), lax.axis_index("cols")
    return row, col, row // (NY * NZ), (row // NZ) % NY, row % NZ


def row_at(x, y, z):
    return (x * NY + y) * NZ + z


def send(src, dst, send_sem, recv_sem, device):
    return pltpu.make_async_remote_copy(
        src_ref=src,
        dst_ref=dst,
        send_sem=send_sem,
        recv_sem=recv_sem,
        device_id=device,
        device_id_type=MESH,
    )


def gather_kernel(
    row_feat, col_feat, ids, w_row, w_col,
    cols_out, rows_out, offset_out,
    ybuf, zbuf, flat, xbuf, rbuf, lbuf,
    ysend, yrecv, zsend, zrecv, xsend, xrecv, rsend, rrecv, lsend, lrecv,
):
    row, col, x, y, z = place()
    has_up, has_down = row > 0, row < NROW - 1
    gives_right = (x == NX - 1) & (y == NY - 1) & (col < NCOL - 1)
    gives_left = (x == 0) & (y == 0) & (col > 0)
    takes_left = (x == NX - 1) & (col > 0)
    takes_right = (x == 0) & (col < NCOL - 1)

    ybuf[NY] = jnp.zeros((1, CH), F32)
    flat[NY * NZ + NZ :, :] = jnp.zeros((CHUNK - NY * NZ - NZ, CH), F32)

    @pl.when(jnp.logical_not(has_up))
    def _():
        rbuf[0] = jnp.zeros((NCOL, TR, CH), BF16)
        lbuf[0] = jnp.full((TR, CH), LOW, BF16)

    @pl.when(jnp.logical_not(has_down))
    def _():
        rbuf[2] = jnp.zeros((NCOL, TR, CH), BF16)
        lbuf[2] = jnp.full((TR, CH), LOW, BF16)

    barrier = pltpu.get_barrier_semaphore()

    def greet(device):
        pl.semaphore_signal(barrier, inc=1, device_id=device, device_id_type=MESH)

    for k in range(1, NY):
        greet((row_at(x, (y + k) % NY, z), col))
    for k in range(1, NX):
        greet((row_at((x + k) % NX, y, z), col))
    for k in range(1, NZ):
        greet((row_at(x, y, (z + k) % NZ), col))
    for k in range(1, NCOL):
        greet((row, (col + k) % NCOL))
    expected = NY - 1 + NX - 1 + NZ - 1 + NCOL - 1

    def when_add(cond, amount):
        return jnp.where(cond, amount, 0).astype(jnp.int32)

    @pl.when(has_up)
    def _():
        for k in range(NCOL):
            greet((row - 1, k))

    @pl.when(has_down)
    def _():
        for k in range(NCOL):
            greet((row + 1, k))

    @pl.when(gives_right)
    def _():
        for k in range(NY):
            greet((row_at(x, k, z), col + 1))

    @pl.when(gives_left)
    def _():
        for k in range(NY):
            greet((row_at(x, k, z), col - 1))

    @pl.when(takes_left)
    def _():
        greet((row_at(x, NY - 1, z), col - 1))

    @pl.when(takes_right)
    def _():
        greet((row_at(x, 0, z), col + 1))

    expected = (
        expected
        + when_add(has_up, NCOL)
        + when_add(has_down, NCOL)
        + when_add(gives_right, NY)
        + when_add(gives_left, NY)
        + when_add(takes_left, 1)
        + when_add(takes_right, 1)
    )

    mine = jnp.dot(col_feat[0], w_col[...], preferred_element_type=F32)
    ybuf[y] = mine.astype(BF16).astype(F32)
    rbuf[1, col] = row_feat[...]
    b = ids[...]
    i = lax.broadcasted_iota(jnp.int32, (TR, TC), 0) + row * TR
    j = lax.broadcasted_iota(jnp.int32, (TR, TC), 1) + col * TC
    forced = jnp.where(b >= 1, STEP * (b + 16) - (j - i) - BASE, LOW).astype(F32)
    least = jnp.max(jnp.max(forced, axis=1, keepdims=True), axis=0, keepdims=True)
    least = jnp.maximum(least, float(LOW))
    lbuf[1] = jnp.broadcast_to(least, (TR, CH)).astype(BF16)

    pl.semaphore_wait(barrier, expected)

    ys = []
    for k in range(1, NY):
        to = (y + k) % NY
        copy = send(ybuf.at[y], ybuf.at[y], ysend.at[k], yrecv.at[y], (row_at(x, to, z), col))
        copy.start()
        ys.append(copy)

    def margin_copies(side, to_col, sem):
        return [
            send(ybuf.at[y], ybuf.at[NY], ysend.at[sem + k], yrecv.at[NY], (row_at(x, k, z), to_col))
            for k in range(NY)
        ]

    @pl.when(gives_right)
    def _():
        for copy in margin_copies(0, col + 1, NY):
            copy.start()

    @pl.when(gives_left)
    def _():
        for copy in margin_copies(0, col - 1, 2 * NY):
            copy.start()

    def row_copies(block, to_row, first, skip):
        return [
            send(
                row_feat, rbuf.at[block, col], rsend.at[block, k], rrecv.at[block, col],
                (to_row, (col + k) % NCOL),
            )
            for k in range(skip, NCOL)
        ]

    own = row_copies(1, row, 0, 1)
    for copy in own:
        copy.start()

    def offset_copy(block, to_row):
        return send(lbuf.at[1], lbuf.at[block], lsend.at[block], lrecv.at[block], (to_row, col))

    @pl.when(has_up)
    def _():
        for copy in row_copies(2, row - 1, 0, 0):
            copy.start()
        offset_copy(2, row - 1).start()

    @pl.when(has_down)
    def _():
        for copy in row_copies(0, row + 1, 0, 0):
            copy.start()
        offset_copy(0, row + 1).start()

    def arrived(ref, sem):
        pltpu.make_async_copy(ref, ref, sem).wait()

    for k in range(1, NY):
        at = (y + k) % NY
        arrived(ybuf.at[at], yrecv.at[at])

    @pl.when(takes_left | takes_right)
    def _():
        arrived(ybuf.at[NY], yrecv.at[NY])

    zs = []
    for k in range(1, NZ):
        to = (z + k) % NZ
        copy = send(ybuf, zbuf.at[z], zsend.at[k], zrecv.at[z], (row_at(x, y, to), col))
        copy.start()
        zs.append(copy)
    zbuf[z] = ybuf[...]

    for k in range(1, NCOL):
        at = (col + k) % NCOL
        arrived(rbuf.at[1, at], rrecv.at[1, at])

    @pl.when(has_up)
    def _():
        for k in range(NCOL):
            arrived(rbuf.at[0, k], rrecv.at[0, k])
        arrived(lbuf.at[0], lrecv.at[0])

    @pl.when(has_down)
    def _():
        for k in range(NCOL):
            arrived(rbuf.at[2, k], rrecv.at[2, k])
        arrived(lbuf.at[2], lrecv.at[2])

    sums = jnp.zeros((3 * TR, CH), F32)
    for k in range(NCOL):
        sums = sums + jnp.dot(
            rbuf[:, k].reshape(3 * TR, CH),
            w_row[k * CH : (k + 1) * CH, :],
            preferred_element_type=F32,
        )
    rows_out[...] = sums.astype(BF16).astype(F32)
    offset_out[...] = jnp.maximum(jnp.maximum(lbuf[0], lbuf[1]), lbuf[2]).astype(F32)[0:8]

    for k in range(1, NZ):
        at = (z + k) % NZ
        arrived(zbuf.at[at], zrecv.at[at])

    for a in range(NY + 1):
        for b in range(NZ):
            flat[a * NZ + b : a * NZ + b + 1, :] = zbuf[b, a]
    xbuf[x] = flat[...].astype(BF16)

    xs = []
    for k in range(1, NX):
        to = (x + k) % NX
        copy = send(xbuf.at[x], xbuf.at[x], xsend.at[k], xrecv.at[x], (row_at(to, y, z), col))
        copy.start()
        xs.append(copy)
    for k in range(1, NX):
        at = (x + k) % NX
        arrived(xbuf.at[at], xrecv.at[at])
    cols_out[...] = xbuf[...].reshape(NX * CHUNK, CH)

    for copy in ys + zs + xs + own:
        copy.wait_send()

    @pl.when(gives_right)
    def _():
        for copy in margin_copies(0, col + 1, NY):
            copy.wait_send()

    @pl.when(gives_left)
    def _():
        for copy in margin_copies(0, col - 1, 2 * NY):
            copy.wait_send()

    @pl.when(has_up)
    def _():
        for copy in row_copies(2, row - 1, 0, 0):
            copy.wait_send()
        offset_copy(2, row - 1).wait_send()

    @pl.when(has_down)
    def _():
        for copy in row_copies(0, row + 1, 0, 0):
            copy.wait_send()
        offset_copy(0, row + 1).wait_send()


def gather(row_feat, col_feat, ids, w_row, w_col):
    vmem = pl.BlockSpec(memory_space=pltpu.VMEM)
    dma = pltpu.SemaphoreType.DMA
    return pl.pallas_call(
        gather_kernel,
        out_shape=(
            jax.ShapeDtypeStruct((NX * CHUNK, CH), BF16),
            jax.ShapeDtypeStruct((3 * TR, CH), F32),
            jax.ShapeDtypeStruct((8, CH), F32),
        ),
        in_specs=[vmem] * 5,
        out_specs=(vmem, vmem, vmem),
        scratch_shapes=[
            pltpu.VMEM((NY + 1, 1, CH), F32),
            pltpu.VMEM((NZ, NY + 1, 1, CH), F32),
            pltpu.VMEM((CHUNK, CH), F32),
            pltpu.VMEM((NX, CHUNK, CH), BF16),
            pltpu.VMEM((3, NCOL, TR, CH), BF16),
            pltpu.VMEM((3, TR, CH), BF16),
            dma((3 * NY,)), dma((NY + 1,)),
            dma((NZ,)), dma((NZ,)),
            dma((NX,)), dma((NX,)),
            dma((3, NCOL)), dma((3, NCOL)),
            dma((3,)), dma((3,)),
        ],
        compiler_params=pltpu.CompilerParams(collective_id=0, has_side_effects=True),
    )(row_feat, col_feat, ids, w_row, w_col)


def gelu(value, half):
    inner = value * (0.7978845608028654 + (0.7978845608028654 * 0.044715) * (value * value))
    return (value * half) * (1.0 + jnp.tanh(inner))


def pair_kernel(
    cols_in, rows_in, offset_in, w_out, bias_table, kernel_one, kernel_two,
    out,
    table, colf, shifted, act0, act1, pair0, pair1,
):
    row, col, _, _, _ = place()
    left = jnp.where(col > 0, 1.0, 0.0).astype(F32)
    right = jnp.where(col < NCOL - 1, 1.0, 0.0).astype(F32)

    spot = lax.broadcasted_iota(jnp.int32, (TAB, CH), 0) + (col * TC - row * TR - 2 - (EXT - 1) + BASE)
    bucket = lax.broadcasted_iota(jnp.int32, (TAB, CH), 1)
    at = spot.astype(F32) + offset_in[0:1, :]
    low = jnp.where(bucket == 0, -1e9, (STEP * (bucket + 16)).astype(F32))
    high = jnp.where(bucket == CH - 1, 1e9, (STEP * (bucket + 17)).astype(F32))
    chosen = jnp.where((at >= low) & (at < high), 1.0, 0.0).astype(BF16)
    table[...] = jnp.dot(chosen, bias_table[...], preferred_element_type=F32)

    take = lax.broadcasted_iota(jnp.int32, (WIDE, NX * CHUNK), 0) - 8
    have = lax.broadcasted_iota(jnp.int32, (WIDE, NX * CHUNK), 1)
    block = NY * NZ
    source = (take // block) * CHUNK + take % block
    source = jnp.where(take < 0, (NX - 1) * CHUNK + block + NZ + take, source)
    source = jnp.where(take >= TC, block + take - TC, source)
    order = jnp.where(source == have, 1.0, 0.0).astype(BF16)
    colf[...] = jnp.dot(order, cols_in[...], preferred_element_type=F32)

    shifted[...] = jnp.zeros_like(shifted)

    def inside(bin):
        return jnp.where((bin >= 0) & (bin < TR * NROW), 0.5, 0.0).astype(F32)

    group = 4

    def first(step, carry):
        base = step * group
        outer = [
            (rows_in[pl.ds(TR - 6 + base + k, 1), :] * colf[...]).astype(BF16) for k in range(group)
        ]
        mixed = jnp.dot(
            jnp.concatenate(outer, axis=0), w_out[...], preferred_element_type=F32
        ).reshape(group, WIDE, CH)
        for k in range(group):
            value = (mixed[k] + table[pl.ds(EXT - 1 - base - k, WIDE), :]).astype(BF16)
            pair0[base + k] = value
            act = gelu(value.astype(F32), inside(row * TR - 6 + base + k))
            shifted[k, 8:16, :] = act[0:8] * left
            shifted[k, 16 : WIDE, :] = act[8 : WIDE - 8]
            shifted[k, WIDE : WIDE + 8, :] = act[WIDE - 8 :] * right
        for k in range(group):
            for q in range(3):
                act0[base + k, :, q * CH : (q + 1) * CH] = shifted[
                    k, 8 + 2 * (q - 1) : 8 + 2 * (q - 1) + WIDE, :
                ].astype(BF16)
        return carry

    lax.fori_loop(0, EXT // group, first, 0)

    def second(step, carry):
        base = step * group
        total = jnp.zeros((group * WIDE, CH), F32)
        for p in range(3):
            total = total + jnp.dot(
                act0[pl.ds(base + 2 * p, group)].reshape(group * WIDE, 3 * CH),
                kernel_one[p],
                preferred_element_type=F32,
            )
        total = total.reshape(group, WIDE, CH)
        for k in range(group):
            value = (pair0[base + 2 + k].astype(F32) + total[k]).astype(BF16).astype(F32)
            pair1[base + k] = value[8 : 8 + TC].astype(BF16)
            act = gelu(value, inside(row * TR - 4 + base + k))
            shifted[k, 8:16, :] = act[0:8] * left
            shifted[k, 16 : WIDE, :] = act[8 : WIDE - 8]
            shifted[k, WIDE : WIDE + 8, :] = act[WIDE - 8 :] * right
        for k in range(group):
            for q in range(3):
                act1[base + k, :, q * CH : (q + 1) * CH] = shifted[
                    k, 16 + 4 * (q - 1) : 16 + 4 * (q - 1) + TC, :
                ].astype(BF16)
        return carry

    lax.fori_loop(0, (TR + 8) // group, second, 0)

    def third(step, carry):
        base = step * group
        total = jnp.zeros((group * TC, CH), F32)
        for p in range(3):
            total = total + jnp.dot(
                act1[pl.ds(base + 4 * p, group)].reshape(group * TC, 3 * CH),
                kernel_two[p],
                preferred_element_type=F32,
            )
        total = total.reshape(group, TC, CH)
        for k in range(group):
            out[base + k] = (pair1[base + 4 + k].astype(F32) + total[k]).astype(BF16)
        return carry

    lax.fori_loop(0, TR // group, third, 0)


def pairs(cols, rows, offset, w_out, bias_table, kernel_one, kernel_two):
    vmem = pl.BlockSpec(memory_space=pltpu.VMEM)
    return pl.pallas_call(
        pair_kernel,
        out_shape=jax.ShapeDtypeStruct((TR, TC, CH), BF16),
        in_specs=[vmem] * 7,
        out_specs=vmem,
        scratch_shapes=[
            pltpu.VMEM((TAB, CH), F32),
            pltpu.VMEM((WIDE, CH), F32),
            pltpu.VMEM((4, WIDE + 16, CH), F32),
            pltpu.VMEM((EXT, WIDE, 3 * CH), BF16),
            pltpu.VMEM((TR + 8, TC, 3 * CH), BF16),
            pltpu.VMEM((EXT, WIDE, CH), BF16),
            pltpu.VMEM((TR + 8, TC, CH), BF16),
        ],
        compiler_params=pltpu.CompilerParams(vmem_limit_bytes=48 * 1024 * 1024),
    )(cols, rows, offset, w_out, bias_table, kernel_one.reshape(3, 3 * CH, CH), kernel_two.reshape(3, 3 * CH, CH))


def per_device(
    row_feat, col_feat, bucket_ids, w_row, w_col, w_out, bias_table, kernel_one, kernel_two
):
    cols, rows, offset = gather(row_feat, col_feat, bucket_ids, w_row, w_col)
    return pairs(cols, rows, offset, w_out, bias_table, kernel_one, kernel_two)


def solution(mesh):
    in_specs = (
        P("rows", "cols"),
        P("cols", "rows", None),
        P("rows", "cols"),
        P(),
        P(),
        P(),
        P(),
        P(),
        P(),
    )
    out_specs = P("rows", "cols", None)
    return jax.shard_map(
        per_device, mesh=mesh, in_specs=in_specs, out_specs=out_specs, check_vma=False
    )
```

time: 627 us -> 49.5 us (0.08)
  the two profiles are of different devices: /device:TPU:1 before, /device:TPU:56 now
where the time goes in v1:
time: 49.5 us; the launch traced here: 49.1 us
  Pallas kernels  44.9 us (91%)
  local copies, waits for them, and re-layouts  4.15 us (8%)
    pallas_call x1, Pallas kernels, gather(): pl.pallas_call(gather_kernel, out_shape=(jax.ShapeDtypeStruct((NX * CHUNK...  33.4 us
    pallas_call x1, Pallas kernels, pairs(): pl.pallas_call(pair_kernel, out_shape=jax.ShapeDtypeStruct((TR, TC, CH),...  11.5 us
    unnamed x14, local copies, waits for them, and re-layouts  4.15 us

profile of v1, /device:TPU:56, one launch (start us, length us, event | category | flops | bytes accessed | tf_op | source)
XLA Modules:
  0.0 49.1 jit_solution(15984746202055783053)
XLA Ops:
  0.0 0.0 copy-start.3
  0.0 0.0 copy-start.4
  0.0 33.4 %shard_map.91 = (bf16[256,128]{1,0:T(8,128)(2,1)}, f32[48,128]{1,0:T(8,128)}, f32[8,128]{1,0:T(8,128)}) custom-call(bf16[16,128]{1,0:T(8,128)(2,1)} %row_feat.1, bf16[1,1,512]{2,1,0:T(2,128)(2,1)} %col_feat.1, s32[16,192]{1,0:T(8,128)} %ids.1, bf16[512,128]{1,0:T(8,128)(2,1)} %w_row.1, bf16[512,128]{1,0:T(8,128)(2,1)} %w_col.1), custom_call_target="tpu_custom_call" | custom-call | tf_op jit(solution)/shard_map/pallas_call | solution.py:286
  33.4 0.0 copy-start.6
  33.4 0.0 copy-done.3
  33.4 0.0 copy-done.4
  33.4 0.6 %copy-done.6 = f32[8,128]{1,0:T(8,128)S(1)} copy-done((f32[8,128]{1,0:T(8,128)S(1)}, f32[8,128]{1,0:T(8,128)}, u32[]{:S(2)}) %copy-start.6) | copy-done | bytes 4120
  34.1 0.0 copy-start
  34.1 1.0 %copy-done = bf16[9,128,128]{2,1,0:T(8,128)(2,1)S(1)} copy-done((bf16[9,128,128]{2,1,0:T(8,128)(2,1)S(1)}, bf16[9,128,128]{2,1,0:T(8,128)(2,1)}, u32[]{:S(2)}) %copy-start) | copy-done | bytes 294936
  35.0 0.0 copy-start.1
  35.0 1.0 %copy-done.1 = bf16[9,128,128]{2,1,0:T(8,128)(2,1)S(1)} copy-done((bf16[9,128,128]{2,1,0:T(8,128)(2,1)S(1)}, bf16[9,128,128]{2,1,0:T(8,128)(2,1)}, u32[]{:S(2)}) %copy-start.1) | copy-done | bytes 294936
  36.0 0.0 copy-start.2
  36.0 0.8 %copy-done.2 = bf16[256,128]{1,0:T(8,128)(2,1)S(1)} copy-done((bf16[256,128]{1,0:T(8,128)(2,1)S(1)}, bf16[256,128]{1,0:T(8,128)(2,1)}, u32[]{:S(2)}) %copy-start.2) | copy-done | bytes 65560
  36.8 0.0 copy-start.5
  36.9 0.7 %copy-done.5 = f32[48,128]{1,0:T(8,128)S(1)} copy-done((f32[48,128]{1,0:T(8,128)S(1)}, f32[48,128]{1,0:T(8,128)}, u32[]{:S(2)}) %copy-start.5) | copy-done | bytes 24600
  37.6 11.5 %shard_map.92 = bf16[16,192,128]{2,1,0:T(8,128)(2,1)} custom-call(bf16[256,128]{1,0:T(8,128)(2,1)S(1)} %copy-done.2, f32[48,128]{1,0:T(8,128)S(1)} %copy-done.5, f32[8,128]{1,0:T(8,128)S(1)} %copy-done.6, bf16[128,128]{1,0:T(8,128)(2,1)S(1)} %copy-done.3, bf16[128,128]{1,0:T(8,128)(2,1)S(1)} %copy-done.4, bf16[3,384,128]{2,1,0:T(8,128)(2,1)S(1)} %bitcast.2, ...), custom_call_target="tpu_custom_call" | custom-call | tf_op jit(solution)/shard_map/pallas_call | solution.py:419
Async XLA Ops:
  0.0 33.4 %copy-start.3 = (bf16[128,128]{1,0:T(8,128)(2,1)S(1)}, bf16[128,128]{1,0:T(8,128)(2,1)}, u32[]{:S(2)}) copy-start(bf16[128,128]{1,0:T(8,128)(2,1)} %w_out.1) | copy-start | bytes 98308
  0.0 33.4 %copy-start.4 = (bf16[128,128]{1,0:T(8,128)(2,1)S(1)}, bf16[128,128]{1,0:T(8,128)(2,1)}, u32[]{:S(2)}) copy-start(bf16[128,128]{1,0:T(8,128)(2,1)} %bias_table.1) | copy-start | bytes 98308
  33.4 0.7 %copy-start.6 = (f32[8,128]{1,0:T(8,128)S(1)}, f32[8,128]{1,0:T(8,128)}, u32[]{:S(2)}) copy-start(f32[8,128]{1,0:T(8,128)} %get-tuple-element.10.offset_in) | copy-start | bytes 12292
  34.1 1.0 %copy-start = (bf16[9,128,128]{2,1,0:T(8,128)(2,1)S(1)}, bf16[9,128,128]{2,1,0:T(8,128)(2,1)}, u32[]{:S(2)}) copy-start(bf16[9,128,128]{2,1,0:T(8,128)(2,1)} %param.16) | copy-start | bytes 884740
  35.0 1.0 %copy-start.1 = (bf16[9,128,128]{2,1,0:T(8,128)(2,1)S(1)}, bf16[9,128,128]{2,1,0:T(8,128)(2,1)}, u32[]{:S(2)}) copy-start(bf16[9,128,128]{2,1,0:T(8,128)(2,1)} %param.17) | copy-start | bytes 884740
  36.0 0.8 %copy-start.2 = (bf16[256,128]{1,0:T(8,128)(2,1)S(1)}, bf16[256,128]{1,0:T(8,128)(2,1)}, u32[]{:S(2)}) copy-start(bf16[256,128]{1,0:T(8,128)(2,1)} %get-tuple-element.8.cols_in) | copy-start | bytes 196612
  36.8 0.7 %copy-start.5 = (f32[48,128]{1,0:T(8,128)S(1)}, f32[48,128]{1,0:T(8,128)}, u32[]{:S(2)}) copy-start(f32[48,128]{1,0:T(8,128)} %get-tuple-element.9.rows_in) | copy-start | bytes 73732

commit v2 on v1

--- a/solution.py
+++ b/solution.py
@@ -44,10 +44,10 @@
 
 
 def gather_kernel(
-    row_feat, col_feat, ids, w_row, w_col,
-    cols_out, rows_out, offset_out,
+    row_feat, col_feat, ids, w_row, w_col, bias_table, w_out_hbm, one_hbm, two_hbm,
+    cols_out, rows_out, table, w_out, kernel_one, kernel_two,
     ybuf, zbuf, flat, xbuf, rbuf, lbuf,
-    ysend, yrecv, zsend, zrecv, xsend, xrecv, rsend, rrecv, lsend, lrecv,
+    ysend, yrecv, zsend, zrecv, xsend, xrecv, rsend, rrecv, lsend, lrecv, weight_sem,
 ):
     row, col, x, y, z = place()
     has_up, has_down = row > 0, row < NROW - 1
@@ -124,6 +124,13 @@
         + when_add(takes_left, 1)
         + when_add(takes_right, 1)
     )
+
+    weights = [
+        pltpu.make_async_copy(src, dst, weight_sem.at[k])
+        for k, (src, dst) in enumerate(((w_out_hbm, w_out), (one_hbm, kernel_one), (two_hbm, kernel_two)))
+    ]
+    for copy in weights:
+        copy.start()
 
     mine = jnp.dot(col_feat[0], w_col[...], preferred_element_type=F32)
     ybuf[y] = mine.astype(BF16).astype(F32)
@@ -232,7 +239,15 @@
             preferred_element_type=F32,
         )
     rows_out[...] = sums.astype(BF16).astype(F32)
-    offset_out[...] = jnp.maximum(jnp.maximum(lbuf[0], lbuf[1]), lbuf[2]).astype(F32)[0:8]
+
+    offset = jnp.maximum(jnp.maximum(lbuf[0], lbuf[1]), lbuf[2]).astype(F32)
+    spot = lax.broadcasted_iota(jnp.int32, (TAB, CH), 0) + (col * TC - row * TR - 2 - (EXT - 1) + BASE)
+    bucket = lax.broadcasted_iota(jnp.int32, (TAB, CH), 1)
+    at = spot.astype(F32) + offset[0:1, :]
+    low = jnp.where(bucket == 0, -1e9, (STEP * (bucket + 16)).astype(F32))
+    high = jnp.where(bucket == CH - 1, 1e9, (STEP * (bucket + 17)).astype(F32))
+    chosen = jnp.where((at >= low) & (at < high), 1.0, 0.0).astype(BF16)
+    table[...] = jnp.dot(chosen, bias_table[...], preferred_element_type=F32)
 
     for k in range(1, NZ):
         at = (z + k) % NZ
@@ -256,6 +271,8 @@
 
     for copy in ys + zs + xs + own:
         copy.wait_send()
+    for copy in weights:
+        copy.wait()
 
     @pl.when(gives_right)
     def _():
@@ -280,18 +297,21 @@
         offset_copy(0, row + 1).wait_send()
 
 
-def gather(row_feat, col_feat, ids, w_row, w_col):
+def gather(row_feat, col_feat, ids, w_row, w_col, bias_table, w_out, kernel_one, kernel_two):
     vmem = pl.BlockSpec(memory_space=pltpu.VMEM)
     dma = pltpu.SemaphoreType.DMA
     return pl.pallas_call(
         gather_kernel,
         out_shape=(
-            jax.ShapeDtypeStruct((NX * CHUNK, CH), BF16),
-            jax.ShapeDtypeStruct((3 * TR, CH), F32),
-            jax.ShapeDtypeStruct((8, CH), F32),
+            pltpu.VMEM((NX * CHUNK, CH), BF16),
+            pltpu.VMEM((3 * TR, CH), F32),
+            pltpu.VMEM((TAB, CH), F32),
+            pltpu.VMEM((CH, CH), BF16),
+            pltpu.VMEM((9, CH, CH), BF16),
+            pltpu.VMEM((9, CH, CH), BF16),
         ),
-        in_specs=[vmem] * 5,
-        out_specs=(vmem, vmem, vmem),
+        in_specs=[vmem] * 6 + [pl.BlockSpec(memory_space=pl.ANY)] * 3,
+        out_specs=(vmem,) * 6,
         scratch_shapes=[
             pltpu.VMEM((NY + 1, 1, CH), F32),
             pltpu.VMEM((NZ, NY + 1, 1, CH), F32),
@@ -304,9 +324,10 @@
             dma((NX,)), dma((NX,)),
             dma((3, NCOL)), dma((3, NCOL)),
             dma((3,)), dma((3,)),
+            dma((3,)),
         ],
         compiler_params=pltpu.CompilerParams(collective_id=0, has_side_effects=True),
-    )(row_feat, col_feat, ids, w_row, w_col)
+    )(row_feat, col_feat, ids, w_row, w_col, bias_table, w_out, kernel_one, kernel_two)
 
 
 def gelu(value, half):
@@ -315,21 +336,13 @@
 
 
 def pair_kernel(
-    cols_in, rows_in, offset_in, w_out, bias_table, kernel_one, kernel_two,
+    cols_in, rows_in, table, w_out, kernel_one, kernel_two,
     out,
-    table, colf, shifted, act0, act1, pair0, pair1,
+    colf, shifted, act0, act1, pair0, pair1,
 ):
     row, col, _, _, _ = place()
     left = jnp.where(col > 0, 1.0, 0.0).astype(F32)
     right = jnp.where(col < NCOL - 1, 1.0, 0.0).astype(F32)
-
-    spot = lax.broadcasted_iota(jnp.int32, (TAB, CH), 0) + (col * TC - row * TR - 2 - (EXT - 1) + BASE)
-    bucket = lax.broadcasted_iota(jnp.int32, (TAB, CH), 1)
-    at = spot.astype(F32) + offset_in[0:1, :]
-    low = jnp.where(bucket == 0, -1e9, (STEP * (bucket + 16)).astype(F32))
-    high = jnp.where(bucket == CH - 1, 1e9, (STEP * (bucket + 17)).astype(F32))
-    chosen = jnp.where((at >= low) & (at < high), 1.0, 0.0).astype(BF16)
-    table[...] = jnp.dot(chosen, bias_table[...], preferred_element_type=F32)
 
     take = lax.broadcasted_iota(jnp.int32, (WIDE, NX * CHUNK), 0) - 8
     have = lax.broadcasted_iota(jnp.int32, (WIDE, NX * CHUNK), 1)
@@ -414,15 +427,14 @@
     lax.fori_loop(0, TR // group, third, 0)
 
 
-def pairs(cols, rows, offset, w_out, bias_table, kernel_one, kernel_two):
+def pairs(cols, rows, table, w_out, kernel_one, kernel_two):
     vmem = pl.BlockSpec(memory_space=pltpu.VMEM)
     return pl.pallas_call(
         pair_kernel,
         out_shape=jax.ShapeDtypeStruct((TR, TC, CH), BF16),
-        in_specs=[vmem] * 7,
+        in_specs=[vmem] * 6,
         out_specs=vmem,
         scratch_shapes=[
-            pltpu.VMEM((TAB, CH), F32),
             pltpu.VMEM((WIDE, CH), F32),
             pltpu.VMEM((4, WIDE + 16, CH), F32),
             pltpu.VMEM((EXT, WIDE, 3 * CH), BF16),
@@ -431,14 +443,16 @@
             pltpu.VMEM((TR + 8, TC, CH), BF16),
         ],
         compiler_params=pltpu.CompilerParams(vmem_limit_bytes=48 * 1024 * 1024),
-    )(cols, rows, offset, w_out, bias_table, kernel_one.reshape(3, 3 * CH, CH), kernel_two.reshape(3, 3 * CH, CH))
+    )(cols, rows, table, w_out, kernel_one.reshape(3, 3 * CH, CH), kernel_two.reshape(3, 3 * CH, CH))
 
 
 def per_device(
     row_feat, col_feat, bucket_ids, w_row, w_col, w_out, bias_table, kernel_one, kernel_two
 ):
-    cols, rows, offset = gather(row_feat, col_feat, bucket_ids, w_row, w_col)
-    return pairs(cols, rows, offset, w_out, bias_table, kernel_one, kernel_two)
+    gathered = gather(
+        row_feat, col_feat, bucket_ids, w_row, w_col, bias_table, w_out, kernel_one, kernel_two
+    )
+    return pairs(*gathered)
 
 
 def solution(mesh):

time: 49.5 us -> 44.4 us (0.90)
  local copies, waits for them, and re-layouts: 4.15 us -> 0 us
  Pallas kernels: 44.9 us -> 44.2 us
    unnamed x14 -> x0, local copies, waits for them, and re-layouts: 4.15 us -> none
    pallas_call x1, Pallas kernels: 33.4 us -> 32.7 us  [gather(): pl.pallas_call(gather_kernel, out_shape=(pltpu.VMEM((NX * CHUNK, CH), BF1...]
where the time goes in v2:
time: 44.4 us; the launch traced here: 44.3 us
  Pallas kernels  44.2 us (100%)
    pallas_call x1, Pallas kernels, gather(): pl.pallas_call(gather_kernel, out_shape=(pltpu.VMEM((NX * CHUNK, CH), BF1...  32.7 us
    pallas_call x1, Pallas kernels, pairs(): pl.pallas_call(pair_kernel, out_shape=jax.ShapeDtypeStruct((TR, TC, CH),...  11.6 us

profile of v2, /device:TPU:56, one launch (start us, length us, event | category | flops | bytes accessed | tf_op | source)
XLA Modules:
  0.0 44.3 jit_solution(7130159335052811180)
XLA Ops:
  0.0 32.7 %shard_map.91 = (bf16[256,128]{1,0:T(8,128)(2,1)S(1)}, f32[48,128]{1,0:T(8,128)S(1)}, f32[240,128]{1,0:T(8,128)S(1)}, bf16[128,128]{1,0:T(8,128)(2,1)S(1)}, bf16...) custom-call(bf16[16,128]{1,0:T(8,128)(2,1)} %row_feat.1, bf16[1,1,512]{2,1,0:T(2,128)(2,1)} %col_feat.1, ...), custom_call_target="tpu_custom_call" | custom-call | tf_op jit(solution)/shard_map/pallas_call | solution.py:303
  32.7 11.6 %shard_map.92 = bf16[16,192,128]{2,1,0:T(8,128)(2,1)} custom-call(bf16[256,128]{1,0:T(8,128)(2,1)S(1)} %get-tuple-element.11.cols_in, f32[48,128]{1,0:T(8,128)S(1)} %get-tuple-element.12.rows_in, f32[240,128]{1,0:T(8,128)S(1)} %get-tuple-element.13.table, bf16[128,128]{1,0:T(8,128)(2,1)S(1)} %get-tuple-element.14.w_out, bf16[3,384,128]{2,1,0:T(8,128)(2,1)S(1)} %bitcast.2, ...), custom_call_target="tpu_custom_call" | custom-call | tf_op jit(solution)/shard_map/pallas_call | solution.py:432

commit v3 on v2

--- a/solution.py
+++ b/solution.py
@@ -43,11 +43,17 @@
     )
 
 
+SIDE = 6
+
+
 def gather_kernel(
-    row_feat, col_feat, ids, w_row, w_col, bias_table, w_out_hbm, one_hbm, two_hbm,
-    cols_out, rows_out, table, w_out, kernel_one, kernel_two,
-    ybuf, zbuf, flat, xbuf, rbuf, lbuf,
-    ysend, yrecv, zsend, zrecv, xsend, xrecv, rsend, rrecv, lsend, lrecv, weight_sem,
+    row_hbm, col_hbm, ids_hbm, w_row_hbm, w_col_hbm, bias_hbm, w_out_hbm, one_hbm, two_hbm,
+    colf, rows_out, table, w_out, kernel_one, kernel_two,
+    col_feat, ids, w_row, w_col, bias_table,
+    ybuf, zbuf, flat, xbuf, rbuf, pbuf, lbuf,
+    load_sem, weight_sem,
+    ysend, yrecv, zsend, zrecv, xsend, xrecv, rsend, rrecv, psend, precv, lsend, lrecv,
+    below, ready, edge,
 ):
     row, col, x, y, z = place()
     has_up, has_down = row > 0, row < NROW - 1
@@ -56,17 +62,26 @@
     takes_left = (x == NX - 1) & (col > 0)
     takes_right = (x == 0) & (col < NCOL - 1)
 
+    loads = [
+        pltpu.make_async_copy(src, dst, load_sem.at[k])
+        for k, (src, dst) in enumerate((
+            (col_hbm, col_feat), (w_col_hbm, w_col), (row_hbm, rbuf.at[col]), (ids_hbm, ids),
+            (w_row_hbm, w_row), (bias_hbm, bias_table),
+        ))
+    ]
+    for copy in loads:
+        copy.start()
+
     ybuf[NY] = jnp.zeros((1, CH), F32)
-    flat[NY * NZ + NZ :, :] = jnp.zeros((CHUNK - NY * NZ - NZ, CH), F32)
 
     @pl.when(jnp.logical_not(has_up))
     def _():
-        rbuf[0] = jnp.zeros((NCOL, TR, CH), BF16)
+        pbuf[0] = jnp.zeros((TR, CH), BF16)
         lbuf[0] = jnp.full((TR, CH), LOW, BF16)
 
     @pl.when(jnp.logical_not(has_down))
     def _():
-        rbuf[2] = jnp.zeros((NCOL, TR, CH), BF16)
+        pbuf[2] = jnp.zeros((TR, CH), BF16)
         lbuf[2] = jnp.full((TR, CH), LOW, BF16)
 
     barrier = pltpu.get_barrier_semaphore()
@@ -76,65 +91,62 @@
 
     for k in range(1, NY):
         greet((row_at(x, (y + k) % NY, z), col))
+    for k in range(1, NCOL):
+        greet((row, (col + k) % NCOL))
+
+    @pl.when(z > 0)
+    def _():
+        greet((row - 1, col))
+
+    @pl.when(z < NZ - 1)
+    def _():
+        greet((row + 1, col))
+
+    @pl.when((z == 0) & has_up)
+    def _():
+        greet((row - 1, col))
+
+    @pl.when(gives_right)
+    def _():
+        for k in range(NY):
+            greet((row_at(x, k, z), col + 1))
+
+    @pl.when(gives_left)
+    def _():
+        for k in range(NY):
+            greet((row_at(x, k, z), col - 1))
+
+    @pl.when(takes_left)
+    def _():
+        greet((row_at(x, NY - 1, z), col - 1))
+
+    @pl.when(takes_right)
+    def _():
+        greet((row_at(x, 0, z), col + 1))
+
     for k in range(1, NX):
         greet((row_at((x + k) % NX, y, z), col))
-    for k in range(1, NZ):
-        greet((row_at(x, y, (z + k) % NZ), col))
-    for k in range(1, NCOL):
-        greet((row, (col + k) % NCOL))
-    expected = NY - 1 + NX - 1 + NZ - 1 + NCOL - 1
 
     def when_add(cond, amount):
         return jnp.where(cond, amount, 0).astype(jnp.int32)
 
-    @pl.when(has_up)
-    def _():
-        for k in range(NCOL):
-            greet((row - 1, k))
-
-    @pl.when(has_down)
-    def _():
-        for k in range(NCOL):
-            greet((row + 1, k))
-
-    @pl.when(gives_right)
-    def _():
-        for k in range(NY):
-            greet((row_at(x, k, z), col + 1))
-
-    @pl.when(gives_left)
-    def _():
-        for k in range(NY):
-            greet((row_at(x, k, z), col - 1))
-
-    @pl.when(takes_left)
-    def _():
-        greet((row_at(x, NY - 1, z), col - 1))
-
-    @pl.when(takes_right)
-    def _():
-        greet((row_at(x, 0, z), col + 1))
-
     expected = (
-        expected
-        + when_add(has_up, NCOL)
-        + when_add(has_down, NCOL)
+        NY - 1 + NX - 1 + NCOL - 1
+        + when_add(z > 0, 1)
+        + when_add(z < NZ - 1, 1)
+        + when_add((z == NZ - 1) & has_down, 1)
         + when_add(gives_right, NY)
         + when_add(gives_left, NY)
         + when_add(takes_left, 1)
         + when_add(takes_right, 1)
     )
 
-    weights = [
-        pltpu.make_async_copy(src, dst, weight_sem.at[k])
-        for k, (src, dst) in enumerate(((w_out_hbm, w_out), (one_hbm, kernel_one), (two_hbm, kernel_two)))
-    ]
-    for copy in weights:
-        copy.start()
-
+    loads[0].wait()
+    loads[1].wait()
     mine = jnp.dot(col_feat[0], w_col[...], preferred_element_type=F32)
     ybuf[y] = mine.astype(BF16).astype(F32)
-    rbuf[1, col] = row_feat[...]
+    loads[2].wait()
+    loads[3].wait()
     b = ids[...]
     i = lax.broadcasted_iota(jnp.int32, (TR, TC), 0) + row * TR
     j = lax.broadcasted_iota(jnp.int32, (TR, TC), 1) + col * TC
@@ -152,7 +164,7 @@
         copy.start()
         ys.append(copy)
 
-    def margin_copies(side, to_col, sem):
+    def margin_copies(to_col, sem):
         return [
             send(ybuf.at[y], ybuf.at[NY], ysend.at[sem + k], yrecv.at[NY], (row_at(x, k, z), to_col))
             for k in range(NY)
@@ -160,41 +172,46 @@
 
     @pl.when(gives_right)
     def _():
-        for copy in margin_copies(0, col + 1, NY):
+        for copy in margin_copies(col + 1, NY):
             copy.start()
 
     @pl.when(gives_left)
     def _():
-        for copy in margin_copies(0, col - 1, 2 * NY):
+        for copy in margin_copies(col - 1, 2 * NY):
             copy.start()
 
-    def row_copies(block, to_row, first, skip):
-        return [
-            send(
-                row_feat, rbuf.at[block, col], rsend.at[block, k], rrecv.at[block, col],
-                (to_row, (col + k) % NCOL),
+    @pl.when(z > 1)
+    def _():
+        pl.semaphore_wait(below, 1)
+
+    @pl.when((z > 0) & (z < NZ - 1))
+    def _():
+        pl.semaphore_signal(below, inc=1, device_id=(row + 1, col), device_id_type=MESH)
+
+    for k in range(NZ - 1):
+        @pl.when(k < z)
+        def _():
+            pl.semaphore_signal(
+                ready.at[z], inc=1, device_id=(row_at(x, y, k), col), device_id_type=MESH
             )
-            for k in range(skip, NCOL)
-        ]
-
-    own = row_copies(1, row, 0, 1)
+
+    @pl.when((z == NZ - 1) & has_down)
+    def _():
+        pl.semaphore_signal(edge, inc=1, device_id=(row + 1, col), device_id_type=MESH)
+
+    own = [
+        send(rbuf.at[col], rbuf.at[col], rsend.at[k], rrecv.at[col], (row, (col + k) % NCOL))
+        for k in range(1, NCOL)
+    ]
     for copy in own:
         copy.start()
 
-    def offset_copy(block, to_row):
-        return send(lbuf.at[1], lbuf.at[block], lsend.at[block], lrecv.at[block], (to_row, col))
-
-    @pl.when(has_up)
-    def _():
-        for copy in row_copies(2, row - 1, 0, 0):
-            copy.start()
-        offset_copy(2, row - 1).start()
-
-    @pl.when(has_down)
-    def _():
-        for copy in row_copies(0, row + 1, 0, 0):
-            copy.start()
-        offset_copy(0, row + 1).start()
+    weights = [
+        pltpu.make_async_copy(src, dst, weight_sem.at[k])
+        for k, (src, dst) in enumerate(((w_out_hbm, w_out), (one_hbm, kernel_one), (two_hbm, kernel_two)))
+    ]
+    for copy in weights:
+        copy.start()
 
     def arrived(ref, sem):
         pltpu.make_async_copy(ref, ref, sem).wait()
@@ -207,38 +224,87 @@
     def _():
         arrived(ybuf.at[NY], yrecv.at[NY])
 
-    zs = []
+    def along(k):
+        return send(ybuf, zbuf.at[z], zsend.at[k], zrecv.at[z], (row_at(x, y, k), col))
+
+    for k in range(NZ - 1):
+        @pl.when(k < z)
+        def _():
+            along(k).start()
+
+    zbuf[z] = ybuf[...]
     for k in range(1, NZ):
-        to = (z + k) % NZ
-        copy = send(ybuf, zbuf.at[z], zsend.at[k], zrecv.at[z], (row_at(x, y, to), col))
-        copy.start()
-        zs.append(copy)
-    zbuf[z] = ybuf[...]
-
+        @pl.when(k > z)
+        def _():
+            pl.semaphore_wait(ready.at[k], 1)
+            along(k).start()
+
+    loads[4].wait()
+    loads[5].wait()
     for k in range(1, NCOL):
         at = (col + k) % NCOL
-        arrived(rbuf.at[1, at], rrecv.at[1, at])
-
-    @pl.when(has_up)
-    def _():
-        for k in range(NCOL):
-            arrived(rbuf.at[0, k], rrecv.at[0, k])
-        arrived(lbuf.at[0], lrecv.at[0])
-
-    @pl.when(has_down)
-    def _():
-        for k in range(NCOL):
-            arrived(rbuf.at[2, k], rrecv.at[2, k])
-        arrived(lbuf.at[2], lrecv.at[2])
-
-    sums = jnp.zeros((3 * TR, CH), F32)
+        arrived(rbuf.at[at], rrecv.at[at])
+    sums = jnp.zeros((TR, CH), F32)
     for k in range(NCOL):
         sums = sums + jnp.dot(
-            rbuf[:, k].reshape(3 * TR, CH),
-            w_row[k * CH : (k + 1) * CH, :],
-            preferred_element_type=F32,
+            rbuf[k], w_row[k * CH : (k + 1) * CH, :], preferred_element_type=F32
         )
-    rows_out[...] = sums.astype(BF16).astype(F32)
+    pbuf[1] = sums.astype(BF16)
+
+    def to_next(block, to_row):
+        return [
+            send(pbuf.at[1], pbuf.at[block], psend.at[block], precv.at[block], (to_row, col)),
+            send(lbuf.at[1], lbuf.at[block], lsend.at[block], lrecv.at[block], (to_row, col)),
+        ]
+
+    @pl.when(has_down)
+    def _():
+        for copy in to_next(0, row + 1):
+            copy.start()
+
+    @pl.when(z > 0)
+    def _():
+        for copy in to_next(2, row - 1):
+            copy.start()
+
+    colf[0:8, :] = jnp.zeros((8, CH), F32)
+    colf[WIDE - 8 : WIDE, :] = jnp.zeros((8, CH), F32)
+    block = NY * NZ
+    flat[block + NZ :, :] = jnp.zeros((CHUNK - block - NZ, CH), F32)
+
+    for k in range(1, NZ):
+        at = (z + k) % NZ
+        arrived(zbuf.at[at], zrecv.at[at])
+
+    for a in range(NY + 1):
+        for b in range(NZ):
+            flat[a * NZ + b : a * NZ + b + 1, :] = zbuf[b, a]
+    xbuf[x] = flat[...].astype(BF16)
+
+    xs = []
+    for k in range(1, NX):
+        to = (x + k) % NX
+        copy = send(xbuf.at[x], xbuf.at[x], xsend.at[k], xrecv.at[x], (row_at(to, y, z), col))
+        copy.start()
+        xs.append(copy)
+
+    @pl.when((z == 0) & has_up)
+    def _():
+        pl.semaphore_wait(edge, 1)
+        for copy in to_next(2, row - 1):
+            copy.start()
+
+    @pl.when(has_up)
+    def _():
+        arrived(pbuf.at[0], precv.at[0])
+        arrived(lbuf.at[0], lrecv.at[0])
+
+    @pl.when(has_down)
+    def _():
+        arrived(pbuf.at[2], precv.at[2])
+        arrived(lbuf.at[2], lrecv.at[2])
+
+    rows_out[...] = pbuf[...].reshape(3 * TR, CH).astype(F32)
 
     offset = jnp.maximum(jnp.maximum(lbuf[0], lbuf[1]), lbuf[2]).astype(F32)
     spot = lax.broadcasted_iota(jnp.int32, (TAB, CH), 0) + (col * TC - row * TR - 2 - (EXT - 1) + BASE)
@@ -248,83 +314,86 @@
     high = jnp.where(bucket == CH - 1, 1e9, (STEP * (bucket + 17)).astype(F32))
     chosen = jnp.where((at >= low) & (at < high), 1.0, 0.0).astype(BF16)
     table[...] = jnp.dot(chosen, bias_table[...], preferred_element_type=F32)
-
-    for k in range(1, NZ):
-        at = (z + k) % NZ
-        arrived(zbuf.at[at], zrecv.at[at])
-
-    for a in range(NY + 1):
-        for b in range(NZ):
-            flat[a * NZ + b : a * NZ + b + 1, :] = zbuf[b, a]
-    xbuf[x] = flat[...].astype(BF16)
-
-    xs = []
-    for k in range(1, NX):
-        to = (x + k) % NX
-        copy = send(xbuf.at[x], xbuf.at[x], xsend.at[k], xrecv.at[x], (row_at(to, y, z), col))
-        copy.start()
-        xs.append(copy)
+    for copy in ys + own:
+        copy.wait_send()
+    for copy in weights:
+        copy.wait()
+    for k in range(NZ):
+        @pl.when(k != z)
+        def _():
+            along(k).wait_send()
+
+    @pl.when(gives_right)
+    def _():
+        for copy in margin_copies(col + 1, NY):
+            copy.wait_send()
+
+    @pl.when(gives_left)
+    def _():
+        for copy in margin_copies(col - 1, 2 * NY):
+            copy.wait_send()
+
+    @pl.when(has_up)
+    def _():
+        for copy in to_next(2, row - 1):
+            copy.wait_send()
+
+    @pl.when(has_down)
+    def _():
+        for copy in to_next(0, row + 1):
+            copy.wait_send()
+
     for k in range(1, NX):
         at = (x + k) % NX
         arrived(xbuf.at[at], xrecv.at[at])
-    cols_out[...] = xbuf[...].reshape(NX * CHUNK, CH)
-
-    for copy in ys + zs + xs + own:
+    for k in range(NX):
+        part = xbuf[k].astype(F32)
+        colf[8 + k * block : 8 + (k + 1) * block, :] = part[0:block]
+        if k == 0:
+            colf[8 + TC : 8 + TC + SIDE, :] = part[block : block + SIDE]
+        if k == NX - 1:
+            colf[8 - SIDE : 8, :] = part[block + NZ - SIDE : block + NZ]
+    for copy in xs:
         copy.wait_send()
-    for copy in weights:
-        copy.wait()
-
-    @pl.when(gives_right)
-    def _():
-        for copy in margin_copies(0, col + 1, NY):
-            copy.wait_send()
-
-    @pl.when(gives_left)
-    def _():
-        for copy in margin_copies(0, col - 1, 2 * NY):
-            copy.wait_send()
-
-    @pl.when(has_up)
-    def _():
-        for copy in row_copies(2, row - 1, 0, 0):
-            copy.wait_send()
-        offset_copy(2, row - 1).wait_send()
-
-    @pl.when(has_down)
-    def _():
-        for copy in row_copies(0, row + 1, 0, 0):
-            copy.wait_send()
-        offset_copy(0, row + 1).wait_send()
 
 
 def gather(row_feat, col_feat, ids, w_row, w_col, bias_table, w_out, kernel_one, kernel_two):
     vmem = pl.BlockSpec(memory_space=pltpu.VMEM)
     dma = pltpu.SemaphoreType.DMA
+    signal = pltpu.SemaphoreType.REGULAR
     return pl.pallas_call(
         gather_kernel,
         out_shape=(
-            pltpu.VMEM((NX * CHUNK, CH), BF16),
+            pltpu.VMEM((WIDE, CH), F32),
             pltpu.VMEM((3 * TR, CH), F32),
             pltpu.VMEM((TAB, CH), F32),
             pltpu.VMEM((CH, CH), BF16),
             pltpu.VMEM((9, CH, CH), BF16),
             pltpu.VMEM((9, CH, CH), BF16),
         ),
-        in_specs=[vmem] * 6 + [pl.BlockSpec(memory_space=pl.ANY)] * 3,
+        in_specs=[pl.BlockSpec(memory_space=pl.ANY)] * 9,
         out_specs=(vmem,) * 6,
         scratch_shapes=[
+            pltpu.VMEM((1, 1, NCOL * CH), BF16),
+            pltpu.VMEM((TR, TC), jnp.int32),
+            pltpu.VMEM((NCOL * CH, CH), BF16),
+            pltpu.VMEM((NCOL * CH, CH), BF16),
+            pltpu.VMEM((CH, CH), BF16),
             pltpu.VMEM((NY + 1, 1, CH), F32),
             pltpu.VMEM((NZ, NY + 1, 1, CH), F32),
             pltpu.VMEM((CHUNK, CH), F32),
             pltpu.VMEM((NX, CHUNK, CH), BF16),
-            pltpu.VMEM((3, NCOL, TR, CH), BF16),
+            pltpu.VMEM((NCOL, TR, CH), BF16),
             pltpu.VMEM((3, TR, CH), BF16),
+            pltpu.VMEM((3, TR, CH), BF16),
+            dma((6,)), dma((3,)),
             dma((3 * NY,)), dma((NY + 1,)),
             dma((NZ,)), dma((NZ,)),
             dma((NX,)), dma((NX,)),
-            dma((3, NCOL)), dma((3, NCOL)),
+            dma((NCOL,)), dma((NCOL,)),
             dma((3,)), dma((3,)),
-            dma((3,)),
+            dma((3,)), dma((3,)),
+            signal, signal((NZ,)), signal,
         ],
         compiler_params=pltpu.CompilerParams(collective_id=0, has_side_effects=True),
     )(row_feat, col_feat, ids, w_row, w_col, bias_table, w_out, kernel_one, kernel_two)
@@ -336,22 +405,13 @@
 
 
 def pair_kernel(
-    cols_in, rows_in, table, w_out, kernel_one, kernel_two,
+    colf, rows_in, table, w_out, kernel_one, kernel_two,
     out,
-    colf, shifted, act0, act1, pair0, pair1,
+    shifted, act0, act1, pair0, pair1,
 ):
     row, col, _, _, _ = place()
     left = jnp.where(col > 0, 1.0, 0.0).astype(F32)
     right = jnp.where(col < NCOL - 1, 1.0, 0.0).astype(F32)
-
-    take = lax.broadcasted_iota(jnp.int32, (WIDE, NX * CHUNK), 0) - 8
-    have = lax.broadcasted_iota(jnp.int32, (WIDE, NX * CHUNK), 1)
-    block = NY * NZ
-    source = (take // block) * CHUNK + take % block
-    source = jnp.where(take < 0, (NX - 1) * CHUNK + block + NZ + take, source)
-    source = jnp.where(take >= TC, block + take - TC, source)
-    order = jnp.where(source == have, 1.0, 0.0).astype(BF16)
-    colf[...] = jnp.dot(order, cols_in[...], preferred_element_type=F32)
 
     shifted[...] = jnp.zeros_like(shifted)
 
@@ -435,7 +495,6 @@
         in_specs=[vmem] * 6,
         out_specs=vmem,
         scratch_shapes=[
-            pltpu.VMEM((WIDE, CH), F32),
             pltpu.VMEM((4, WIDE + 16, CH), F32),
             pltpu.VMEM((EXT, WIDE, 3 * CH), BF16),
             pltpu.VMEM((TR + 8, TC, 3 * CH), BF16),

time: 44.4 us -> 42.2 us (0.950)
  the two profiles are of different devices: /device:TPU:56 before, /device:TPU:6 now
where the time goes in v3:
time: 42.2 us; the launch traced here: 42.1 us
  Pallas kernels  42 us (100%)
    pallas_call x1, Pallas kernels, gather(): pl.pallas_call(gather_kernel, out_shape=(pltpu.VMEM((WIDE, CH), F32), plt...  30.7 us
    pallas_call x1, Pallas kernels, pairs(): pl.pallas_call(pair_kernel, out_shape=jax.ShapeDtypeStruct((TR, TC, CH),...  11.3 us

profile of v3, /device:TPU:6, one launch (start us, length us, event | category | flops | bytes accessed | tf_op | source)
XLA Modules:
  0.0 42.1 jit_solution(7391374501171395468)
XLA Ops:
  0.0 30.7 %shard_map.91 = (f32[208,128]{1,0:T(8,128)S(1)}, f32[48,128]{1,0:T(8,128)S(1)}, f32[240,128]{1,0:T(8,128)S(1)}, bf16[128,128]{1,0:T(8,128)(2,1)S(1)}, bf16[9,128...) custom-call(bf16[16,128]{1,0:T(8,128)(2,1)} %row_hbm.1, bf16[1,1,512]{2,1,0:T(2,128)(2,1)} %col_hbm.1, ...), custom_call_target="tpu_custom_call" | custom-call | tf_op jit(solution)/shard_map/pallas_call | solution.py:364
  30.7 11.3 %shard_map.92 = bf16[16,192,128]{2,1,0:T(8,128)(2,1)} custom-call(f32[208,128]{1,0:T(8,128)S(1)} %get-tuple-element.11.colf, f32[48,128]{1,0:T(8,128)S(1)} %get-tuple-element.12.rows_in, f32[240,128]{1,0:T(8,128)S(1)} %get-tuple-element.13.table, bf16[128,128]{1,0:T(8,128)(2,1)S(1)} %get-tuple-element.14.w_out, bf16[3,384,128]{2,1,0:T(8,128)(2,1)S(1)} %bitcast.2, ...), custom_call_target="tpu_custom_call" | custom-call | tf_op jit(solution)/shard_map/pallas_call | solution.py:492

commit v4 on v3

--- a/solution.py
+++ b/solution.py
@@ -446,13 +446,14 @@
 
     def second(step, carry):
         base = step * group
-        total = jnp.zeros((group * WIDE, CH), F32)
-        for p in range(3):
-            total = total + jnp.dot(
-                act0[pl.ds(base + 2 * p, group)].reshape(group * WIDE, 3 * CH),
-                kernel_one[p],
-                preferred_element_type=F32,
-            )
+        total = jnp.dot(
+            jnp.concatenate(
+                [act0[pl.ds(base + 2 * p, group)].reshape(group * WIDE, 3 * CH) for p in range(3)],
+                axis=1,
+            ),
+            kernel_one[...].reshape(9 * CH, CH),
+            preferred_element_type=F32,
+        )
         total = total.reshape(group, WIDE, CH)
         for k in range(group):
             value = (pair0[base + 2 + k].astype(F32) + total[k]).astype(BF16).astype(F32)
@@ -472,13 +473,14 @@
 
     def third(step, carry):
         base = step * group
-        total = jnp.zeros((group * TC, CH), F32)
-        for p in range(3):
-            total = total + jnp.dot(
-                act1[pl.ds(base + 4 * p, group)].reshape(group * TC, 3 * CH),
-                kernel_two[p],
-                preferred_element_type=F32,
-            )
+        total = jnp.dot(
+            jnp.concatenate(
+                [act1[pl.ds(base + 4 * p, group)].reshape(group * TC, 3 * CH) for p in range(3)],
+                axis=1,
+            ),
+            kernel_two[...].reshape(9 * CH, CH),
+            preferred_element_type=F32,
+        )
         total = total.reshape(group, TC, CH)
         for k in range(group):
             out[base + k] = (pair1[base + 4 + k].astype(F32) + total[k]).astype(BF16)

time: 42.2 us -> 42.2 us (level)
  no operation moved by 1% of the time
where the time goes in v4:
time: 42.2 us; the launch traced here: 42.1 us
  Pallas kernels  42.1 us (100%)
    pallas_call x1, Pallas kernels, gather(): pl.pallas_call(gather_kernel, out_shape=(pltpu.VMEM((WIDE, CH), F32), plt...  30.7 us
    pallas_call x1, Pallas kernels, pairs(): pl.pallas_call(pair_kernel, out_shape=jax.ShapeDtypeStruct((TR, TC, CH),...  11.4 us

profile of v4, /device:TPU:6, one launch (start us, length us, event | category | flops | bytes accessed | tf_op | source)
XLA Modules:
  0.0 42.1 jit_solution(8054251419863743069)
XLA Ops:
  0.0 30.7 %shard_map.91 = (f32[208,128]{1,0:T(8,128)S(1)}, f32[48,128]{1,0:T(8,128)S(1)}, f32[240,128]{1,0:T(8,128)S(1)}, bf16[128,128]{1,0:T(8,128)(2,1)S(1)}, bf16[9,128...) custom-call(bf16[16,128]{1,0:T(8,128)(2,1)} %row_hbm.1, bf16[1,1,512]{2,1,0:T(2,128)(2,1)} %col_hbm.1, ...), custom_call_target="tpu_custom_call" | custom-call | tf_op jit(solution)/shard_map/pallas_call | solution.py:364
  30.7 11.4 %shard_map.92 = bf16[16,192,128]{2,1,0:T(8,128)(2,1)} custom-call(f32[208,128]{1,0:T(8,128)S(1)} %get-tuple-element.11.colf, f32[48,128]{1,0:T(8,128)S(1)} %get-tuple-element.12.rows_in, f32[240,128]{1,0:T(8,128)S(1)} %get-tuple-element.13.table, bf16[128,128]{1,0:T(8,128)(2,1)S(1)} %get-tuple-element.14.w_out, bf16[3,384,128]{2,1,0:T(8,128)(2,1)S(1)} %bitcast.2, ...), custom_call_target="tpu_custom_call" | custom-call | tf_op jit(solution)/shard_map/pallas_call | solution.py:494

commit v5 on v3

--- a/solution.py
+++ b/solution.py
@@ -15,6 +15,7 @@
 NROW, NCOL = NX * NY * NZ, 4
 TR, TC, CH = 16, 192, 128
 STEP = 24
+GROUP = 4
 BASE = 3072
 LOW = -240
 EXT = 28
@@ -48,7 +49,7 @@
 
 def gather_kernel(
     row_hbm, col_hbm, ids_hbm, w_row_hbm, w_col_hbm, bias_hbm, w_out_hbm, one_hbm, two_hbm,
-    colf, rows_out, table, w_out, kernel_one, kernel_two,
+    colf, rows_out, table, w_out, one_wide, one_narrow, two_wide, two_narrow,
     col_feat, ids, w_row, w_col, bias_table,
     ybuf, zbuf, flat, xbuf, rbuf, pbuf, lbuf,
     load_sem, weight_sem,
@@ -206,9 +207,17 @@
     for copy in own:
         copy.start()
 
+    layout = [(w_out_hbm, w_out)]
+    for taps, wide, narrow in ((one_hbm, one_wide, one_narrow), (two_hbm, two_wide, two_narrow)):
+        wide[3 * CH :, 0:CH] = jnp.zeros((CH, CH), BF16)
+        for p in range(3):
+            for q in range(2):
+                layout.append((taps.at[3 * p + q], wide.at[p * CH : (p + 1) * CH, q * CH : (q + 1) * CH]))
+        layout.append((taps.at[8], wide.at[3 * CH :, CH:]))
+        for p in range(2):
+            layout.append((taps.at[3 * p + 2], narrow.at[p * CH : (p + 1) * CH]))
     weights = [
-        pltpu.make_async_copy(src, dst, weight_sem.at[k])
-        for k, (src, dst) in enumerate(((w_out_hbm, w_out), (one_hbm, kernel_one), (two_hbm, kernel_two)))
+        pltpu.make_async_copy(src, dst, weight_sem.at[k]) for k, (src, dst) in enumerate(layout)
     ]
     for copy in weights:
         copy.start()
@@ -368,11 +377,13 @@
             pltpu.VMEM((3 * TR, CH), F32),
             pltpu.VMEM((TAB, CH), F32),
             pltpu.VMEM((CH, CH), BF16),
-            pltpu.VMEM((9, CH, CH), BF16),
-            pltpu.VMEM((9, CH, CH), BF16),
+            pltpu.VMEM((4 * CH, 2 * CH), BF16),
+            pltpu.VMEM((2 * CH, CH), BF16),
+            pltpu.VMEM((4 * CH, 2 * CH), BF16),
+            pltpu.VMEM((2 * CH, CH), BF16),
         ),
         in_specs=[pl.BlockSpec(memory_space=pl.ANY)] * 9,
-        out_specs=(vmem,) * 6,
+        out_specs=(vmem,) * 8,
         scratch_shapes=[
             pltpu.VMEM((1, 1, NCOL * CH), BF16),
             pltpu.VMEM((TR, TC), jnp.int32),
@@ -386,7 +397,7 @@
             pltpu.VMEM((NCOL, TR, CH), BF16),
             pltpu.VMEM((3, TR, CH), BF16),
             pltpu.VMEM((3, TR, CH), BF16),
-            dma((6,)), dma((3,)),
+            dma((6,)), dma((19,)),
             dma((3 * NY,)), dma((NY + 1,)),
             dma((NZ,)), dma((NZ,)),
             dma((NX,)), dma((NX,)),
@@ -405,104 +416,99 @@
 
 
 def pair_kernel(
-    colf, rows_in, table, w_out, kernel_one, kernel_two,
+    colf, rows_in, table, w_out, one_wide, one_narrow, two_wide, two_narrow,
     out,
-    shifted, act0, act1, pair0, pair1,
+    shifted, moved, act0, act1, pair0, pair1,
 ):
     row, col, _, _, _ = place()
     left = jnp.where(col > 0, 1.0, 0.0).astype(F32)
     right = jnp.where(col < NCOL - 1, 1.0, 0.0).astype(F32)
-
-    shifted[...] = jnp.zeros_like(shifted)
+    edge = jnp.zeros((GROUP, 8, CH), F32)
+    shifted[:, WIDE:, :] = edge
+    moved[:, 0:8, :] = edge
 
     def inside(bin):
         return jnp.where((bin >= 0) & (bin < TR * NROW), 0.5, 0.0).astype(F32)
 
-    group = 4
+    def keep(acts, k, at, value, half, gap):
+        act = gelu(value, half)
+        act = jnp.concatenate([act[0:8] * left, act[8 : WIDE - 8], act[WIDE - 8 :] * right], axis=0)
+        shifted[k, 0:WIDE, :] = act
+        acts[at, :, 0:CH] = act.astype(BF16)
+        acts[at, :, CH:] = shifted[k, gap : gap + WIDE, :].astype(BF16)
+
+    def convolve(acts, base, gap, wide, narrow):
+        tops = [acts[pl.ds(base + gap * p, GROUP)].reshape(GROUP * WIDE, 2 * CH) for p in range(3)]
+        both = jnp.dot(
+            jnp.concatenate([tops[0][:, 0:CH], tops[1][:, 0:CH], tops[2]], axis=1),
+            wide[...],
+            preferred_element_type=F32,
+        )
+        last = jnp.dot(
+            jnp.concatenate([tops[0][:, CH:], tops[1][:, CH:]], axis=1),
+            narrow[...],
+            preferred_element_type=F32,
+        )
+        moved[:, 8:, :] = both[:, 0:CH].reshape(GROUP, WIDE, CH)
+        return (both[:, CH:] + last).reshape(GROUP, WIDE, CH)
 
     def first(step, carry):
-        base = step * group
+        base = step * GROUP
         outer = [
-            (rows_in[pl.ds(TR - 6 + base + k, 1), :] * colf[...]).astype(BF16) for k in range(group)
+            (rows_in[pl.ds(TR - 6 + base + k, 1), :] * colf[...]).astype(BF16) for k in range(GROUP)
         ]
         mixed = jnp.dot(
             jnp.concatenate(outer, axis=0), w_out[...], preferred_element_type=F32
-        ).reshape(group, WIDE, CH)
-        for k in range(group):
+        ).reshape(GROUP, WIDE, CH)
+        for k in range(GROUP):
             value = (mixed[k] + table[pl.ds(EXT - 1 - base - k, WIDE), :]).astype(BF16)
             pair0[base + k] = value
-            act = gelu(value.astype(F32), inside(row * TR - 6 + base + k))
-            shifted[k, 8:16, :] = act[0:8] * left
-            shifted[k, 16 : WIDE, :] = act[8 : WIDE - 8]
-            shifted[k, WIDE : WIDE + 8, :] = act[WIDE - 8 :] * right
-        for k in range(group):
-            for q in range(3):
-                act0[base + k, :, q * CH : (q + 1) * CH] = shifted[
-                    k, 8 + 2 * (q - 1) : 8 + 2 * (q - 1) + WIDE, :
-                ].astype(BF16)
+            keep(act0, k, base + k, value.astype(F32), inside(row * TR - 6 + base + k), 2)
         return carry
 
-    lax.fori_loop(0, EXT // group, first, 0)
+    lax.fori_loop(0, EXT // GROUP, first, 0)
 
     def second(step, carry):
-        base = step * group
-        total = jnp.zeros((group * WIDE, CH), F32)
-        for p in range(3):
-            total = total + jnp.dot(
-                act0[pl.ds(base + 2 * p, group)].reshape(group * WIDE, 3 * CH),
-                kernel_one[p],
-                preferred_element_type=F32,
-            )
-        total = total.reshape(group, WIDE, CH)
-        for k in range(group):
-            value = (pair0[base + 2 + k].astype(F32) + total[k]).astype(BF16).astype(F32)
-            pair1[base + k] = value[8 : 8 + TC].astype(BF16)
-            act = gelu(value, inside(row * TR - 4 + base + k))
-            shifted[k, 8:16, :] = act[0:8] * left
-            shifted[k, 16 : WIDE, :] = act[8 : WIDE - 8]
-            shifted[k, WIDE : WIDE + 8, :] = act[WIDE - 8 :] * right
-        for k in range(group):
-            for q in range(3):
-                act1[base + k, :, q * CH : (q + 1) * CH] = shifted[
-                    k, 16 + 4 * (q - 1) : 16 + 4 * (q - 1) + TC, :
-                ].astype(BF16)
+        base = step * GROUP
+        total = convolve(act0, base, 2, one_wide, one_narrow)
+        for k in range(GROUP):
+            value = (
+                pair0[base + 2 + k].astype(F32) + (total[k] + moved[k, 6 : 6 + WIDE, :])
+            ).astype(BF16)
+            pair1[base + k] = value
+            keep(act1, k, base + k, value.astype(F32), inside(row * TR - 4 + base + k), 4)
         return carry
 
-    lax.fori_loop(0, (TR + 8) // group, second, 0)
+    lax.fori_loop(0, (TR + 8) // GROUP, second, 0)
 
     def third(step, carry):
-        base = step * group
-        total = jnp.zeros((group * TC, CH), F32)
-        for p in range(3):
-            total = total + jnp.dot(
-                act1[pl.ds(base + 4 * p, group)].reshape(group * TC, 3 * CH),
-                kernel_two[p],
-                preferred_element_type=F32,
-            )
-        total = total.reshape(group, TC, CH)
-        for k in range(group):
-            out[base + k] = (pair1[base + 4 + k].astype(F32) + total[k]).astype(BF16)
+        base = step * GROUP
+        total = convolve(act1, base, 4, two_wide, two_narrow)
+        for k in range(GROUP):
+            value = pair1[base + 4 + k].astype(F32)[8 : 8 + TC]
+            out[base + k] = (value + (total[k, 8 : 8 + TC] + moved[k, 12 : 12 + TC, :])).astype(BF16)
         return carry
 
-    lax.fori_loop(0, TR // group, third, 0)
-
-
-def pairs(cols, rows, table, w_out, kernel_one, kernel_two):
+    lax.fori_loop(0, TR // GROUP, third, 0)
+
+
+def pairs(*gathered):
     vmem = pl.BlockSpec(memory_space=pltpu.VMEM)
     return pl.pallas_call(
         pair_kernel,
         out_shape=jax.ShapeDtypeStruct((TR, TC, CH), BF16),
-        in_specs=[vmem] * 6,
+        in_specs=[vmem] * 8,
         out_specs=vmem,
         scratch_shapes=[
-            pltpu.VMEM((4, WIDE + 16, CH), F32),
-            pltpu.VMEM((EXT, WIDE, 3 * CH), BF16),
-            pltpu.VMEM((TR + 8, TC, 3 * CH), BF16),
+            pltpu.VMEM((GROUP, WIDE + 8, CH), F32),
+            pltpu.VMEM((GROUP, WIDE + 8, CH), F32),
+            pltpu.VMEM((EXT, WIDE, 2 * CH), BF16),
+            pltpu.VMEM((TR + 8, WIDE, 2 * CH), BF16),
             pltpu.VMEM((EXT, WIDE, CH), BF16),
-            pltpu.VMEM((TR + 8, TC, CH), BF16),
+            pltpu.VMEM((TR + 8, WIDE, CH), BF16),
         ],
         compiler_params=pltpu.CompilerParams(vmem_limit_bytes=48 * 1024 * 1024),
-    )(cols, rows, table, w_out, kernel_one.reshape(3, 3 * CH, CH), kernel_two.reshape(3, 3 * CH, CH))
+    )(*gathered)
 
 
 def per_device(

time: 42.2 us -> 40.8 us (0.967)
  Pallas kernels: 42 us -> 40.6 us
    pallas_call x1, Pallas kernels: 11.3 us -> 9.74 us  [pairs(): pl.pallas_call(pair_kernel, out_shape=jax.ShapeDtypeStruct((TR, TC, CH),...]
where the time goes in v5:
time: 40.8 us; the launch traced here: 40.6 us
  Pallas kernels  40.6 us (100%)
    pallas_call x1, Pallas kernels, gather(): pl.pallas_call(gather_kernel, out_shape=(pltpu.VMEM((WIDE, CH), F32), plt...  30.9 us
    pallas_call x1, Pallas kernels, pairs(): pl.pallas_call(pair_kernel, out_shape=jax.ShapeDtypeStruct((TR, TC, CH),...  9.74 us

profile of v5, /device:TPU:6, one launch (start us, length us, event | category | flops | bytes accessed | tf_op | source)
XLA Modules:
  0.0 40.6 jit_solution(5092507854049866745)
XLA Ops:
  0.0 30.9 %shard_map.91 = (f32[208,128]{1,0:T(8,128)S(1)}, f32[48,128]{1,0:T(8,128)S(1)}, f32[240,128]{1,0:T(8,128)S(1)}, bf16[128,128]{1,0:T(8,128)(2,1)S(1)}, bf16[512,2...) custom-call(bf16[16,128]{1,0:T(8,128)(2,1)} %row_hbm.1, ...), custom_call_target="tpu_custom_call" | custom-call | tf_op jit(solution)/shard_map/pallas_call | solution.py:373
  30.9 9.7 %shard_map.92 = bf16[16,192,128]{2,1,0:T(8,128)(2,1)} custom-call(f32[208,128]{1,0:T(8,128)S(1)} %get-tuple-element.13.colf, f32[48,128]{1,0:T(8,128)S(1)} %get-tuple-element.14.rows_in, f32[240,128]{1,0:T(8,128)S(1)} %get-tuple-element.15.table, bf16[128,128]{1,0:T(8,128)(2,1)S(1)} %get-tuple-element.16.w_out, ...), custom_call_target="tpu_custom_call" | custom-call | tf_op jit(solution)/shard_map/pallas_call | solution.py:497
